TPU v7x, 32 devices: a whole 2x2x4 slice. The times are simulated.
32 devices in a mesh: rep: 8 (over z, x), shard: 4 (over y, core).
Axes of the slice: x: 2, y: 2, z: 4, core: 2. Of those that a mesh axis runs over, the one named last changes fastest.
Arguments:
- hidden_in: bfloat16 [8, 512, 960], P('rep', 'shard'), may hold values from -6 to 6
- out_grad: bfloat16 [8, 512, 960], P('rep', 'shard'), may hold values from -6 to 6
- norm1_gain: bfloat16 [960], P('shard'), may hold values from 0.5 to 1.5
- q_weight: bfloat16 [960, 960], P('shard'), may hold values from -0.1875 to 0.1875
- k_weight: bfloat16 [960, 320], P('shard'), may hold values from -0.1875 to 0.1875
- v_weight: bfloat16 [960, 320], P('shard'), may hold values from -0.1875 to 0.1875
- o_weight: bfloat16 [960, 960], P(None, 'shard'), may hold values from -1.5 to 1.5
- norm2_gain: bfloat16 [960], P('shard'), may hold values from 0.5 to 1.5
- gate_weight: bfloat16 [960, 2560], P('shard'), may hold values from -0.1875 to 0.1875
- up_weight: bfloat16 [960, 2560], P('shard'), may hold values from -0.1875 to 0.1875
- down_weight: bfloat16 [2560, 960], P('shard'), may hold values from -0.125 to 0.125
Outputs:
- output: float32 [8, 512, 960], P('rep', 'shard')
- input_grad: float32 [8, 512, 960], P('rep', 'shard')
- norm1_gain_grad: float32 [960], P('shard')
- q_weight_grad: float32 [960, 960], P('shard')
- k_weight_grad: float32 [960, 320], P('shard')
- v_weight_grad: float32 [960, 320], P('shard')
- o_weight_grad: float32 [960, 960], P(None, 'shard')
- norm2_gain_grad: float32 [960], P('shard')
- gate_weight_grad: float32 [960, 2560], P('shard')
- up_weight_grad: float32 [960, 2560], P('shard')
- down_weight_grad: float32 [2560, 960], P('shard')
All inputs are finite; a program needn't handle non-finite values.
Results may differ from a plain program's by a relative error of at most 0.02.
Values may be sent and summed in bfloat16 or wider, within the bound.
No kernel may reach another device: no remote copies, remote signals or barrier semaphores. Data moves between devices by JAX's collectives and lax.ppermute only.
A program may use at most 192 MiB of HBM per device.

v0:
```python
from functools import partial
import jax
import jax.numpy as jnp
from jax import lax
from jax.sharding import PartitionSpec as P

HQ = 15
KEY_VALUE_HEADS = 5
HEAD_SIZE = 64
QD = 960
KVD = 320
QUERY_PER_KV = 3
EPSILON = 1e-05
SCALE = 0.125
NEGATIVE = -1e30
THETA = 10000.0


def rms_inverse(rows):
    return lax.rsqrt(jnp.mean(rows * rows, axis=-1, keepdims=True) + EPSILON)


def rope_tables(positions):
    half = HEAD_SIZE // 2
    freqs = THETA ** (-(jnp.arange(half, dtype=jnp.float32) * 2.0 / HEAD_SIZE))
    angles = positions.astype(jnp.float32)[:, None] * freqs[None, :]
    return (jnp.cos(angles)[:, None, :], jnp.sin(angles)[:, None, :])


def rotate(tensor, cosine_table, sine_table):
    half = HEAD_SIZE // 2
    first, second = (tensor[..., :half], tensor[..., half:])
    return jnp.concatenate(
        [first * cosine_table - second * sine_table, second * cosine_table + first * sine_table],
        axis=-1,
    )


def inverse_rotary(tensor, cosine_table, sine_table):
    half = HEAD_SIZE // 2
    first, second = (tensor[..., :half], tensor[..., half:])
    return jnp.concatenate(
        [first * cosine_table + second * sine_table, second * cosine_table - first * sine_table],
        axis=-1,
    )


def head_scores(query_rows, keys, query_pos, key_pos):
    scores = jnp.einsum("ngd,ld->gnl", query_rows, keys, preferred_element_type=jnp.float32) * SCALE
    allowed = key_pos[None, None, :] <= query_pos[None, :, None]
    return (jnp.where(allowed, scores, NEGATIVE), allowed)


def head_forward(inputs, query_pos, key_pos):
    query_rows, keys, value_rows = inputs
    scores, allowed = head_scores(query_rows, keys, query_pos, key_pos)
    log_total = jax.nn.logsumexp(scores, axis=-1)
    probs = jnp.where(allowed, jnp.exp(scores - log_total[..., None]), 0.0)
    attended_rows = jnp.einsum(
        "gnl,ld->ngd", probs.astype(jnp.bfloat16), value_rows, preferred_element_type=jnp.float32
    )
    return (attended_rows, log_total)


def head_backward(inputs, query_pos, key_pos):
    query_rows, keys, value_rows, log_total, attention_gradient, attended_rows = inputs
    scores, allowed = head_scores(query_rows, keys, query_pos, key_pos)
    probs = jnp.where(allowed, jnp.exp(scores - log_total[..., None]), 0.0)
    probs_b = probs.astype(jnp.bfloat16)
    value_grad = jnp.einsum(
        "gnl,ngd->ld", probs_b, attention_gradient, preferred_element_type=jnp.float32
    )
    grad_prob = jnp.einsum(
        "ngd,ld->gnl", attention_gradient, value_rows, preferred_element_type=jnp.float32
    )
    delta = jnp.transpose(
        jnp.sum(attention_gradient.astype(jnp.float32) * attended_rows.astype(jnp.float32), axis=-1)
    )
    grad_score = (probs * (grad_prob - delta[..., None]) * SCALE).astype(jnp.bfloat16)
    query_grad = jnp.einsum("gnl,ld->ngd", grad_score, keys, preferred_element_type=jnp.float32)
    key_grad = jnp.einsum("gnl,ngd->ld", grad_score, query_rows, preferred_element_type=jnp.float32)
    return (query_grad, key_grad, value_grad)


def outer(left, right):
    return lax.dot_general(
        left, right, (((0,), (0,)), ((), ())), preferred_element_type=jnp.float32
    )


def back(left, weight):
    return lax.dot_general(
        left, weight, (((1,), (1,)), ((), ())), preferred_element_type=jnp.float32
    )


def local(
    hidden_in,
    out_grad,
    norm1_gain,
    q_weight,
    k_weight,
    v_weight,
    o_weight,
    norm2_gain,
    gate_weight,
    up_weight,
    down_weight,
):
    params = (
        lax.all_gather(norm1_gain, "shard", axis=0, tiled=True),
        lax.all_gather(q_weight, "shard", axis=0, tiled=True),
        lax.all_gather(k_weight, "shard", axis=0, tiled=True),
        lax.all_gather(v_weight, "shard", axis=0, tiled=True),
        lax.all_gather(o_weight, "shard", axis=1, tiled=True),
        lax.all_gather(norm2_gain, "shard", axis=0, tiled=True),
        lax.all_gather(gate_weight, "shard", axis=0, tiled=True),
        lax.all_gather(up_weight, "shard", axis=0, tiled=True),
        lax.all_gather(down_weight, "shard", axis=0, tiled=True),
    )
    gain_one, w_query, key_matrix, value_matrix, w_out, gain_two, w_gate, w_up, w_down = params
    token_count = hidden_in.shape[1]
    sequence_length_total = token_count * lax.axis_size("shard")
    query_pos = lax.axis_index("shard") * token_count + jnp.arange(token_count, dtype=jnp.int32)
    key_pos = jnp.arange(sequence_length_total, dtype=jnp.int32)
    x_full = hidden_in[0].astype(jnp.float32)
    inv_one = rms_inverse(x_full)
    normed_one = x_full * inv_one
    gain_one_f = gain_one.astype(jnp.float32)
    first_input = (normed_one * gain_one_f).astype(jnp.bfloat16)
    cosine_table, sine_table = rope_tables(query_pos)
    query_raw = jnp.dot(first_input, w_query, preferred_element_type=jnp.float32).reshape(
        token_count, HQ, HEAD_SIZE
    )
    query_rows = rotate(query_raw, cosine_table, sine_table).astype(jnp.bfloat16)
    unrotated_key = jnp.dot(first_input, key_matrix, preferred_element_type=jnp.float32).reshape(
        token_count, KEY_VALUE_HEADS, HEAD_SIZE
    )
    keys_own = (
        rotate(unrotated_key, cosine_table, sine_table)
        .astype(jnp.bfloat16)
        .reshape(token_count, KVD)
    )
    values_own = jnp.dot(first_input, value_matrix, preferred_element_type=jnp.float32).astype(
        jnp.bfloat16
    )
    gathered_keys, gathered_values = (
        lax.all_gather(keys_own, "shard", axis=0, tiled=True),
        lax.all_gather(values_own, "shard", axis=0, tiled=True),
    )
    query_head_rows = jnp.transpose(
        query_rows.reshape(token_count, KEY_VALUE_HEADS, QUERY_PER_KV, HEAD_SIZE), (1, 0, 2, 3)
    )
    key_head_rows = jnp.transpose(
        gathered_keys.reshape(sequence_length_total, KEY_VALUE_HEADS, HEAD_SIZE), (1, 0, 2)
    )
    value_head_rows = jnp.transpose(
        gathered_values.reshape(sequence_length_total, KEY_VALUE_HEADS, HEAD_SIZE), (1, 0, 2)
    )
    att_heads, log_total = lax.map(
        partial(head_forward, query_pos=query_pos, key_pos=key_pos),
        (query_head_rows, key_head_rows, value_head_rows),
    )
    attended_rows = (
        jnp.transpose(att_heads, (1, 0, 2, 3)).reshape(token_count, QD).astype(jnp.bfloat16)
    )
    x_one = x_full + jnp.dot(attended_rows, w_out, preferred_element_type=jnp.float32)
    inv_two = rms_inverse(x_one)
    normed_two = x_one * inv_two
    gain_two_f = gain_two.astype(jnp.float32)
    input_two = (normed_two * gain_two_f).astype(jnp.bfloat16)
    gate = jnp.dot(input_two, w_gate, preferred_element_type=jnp.float32)
    upward = jnp.dot(input_two, w_up, preferred_element_type=jnp.float32)
    sigma = jax.nn.sigmoid(gate)
    silu_gate = gate * sigma
    hidden_act = (silu_gate * upward).astype(jnp.bfloat16)
    output = x_one + jnp.dot(hidden_act, w_down, preferred_element_type=jnp.float32)
    params = (
        lax.all_gather(norm1_gain, "shard", axis=0, tiled=True),
        lax.all_gather(q_weight, "shard", axis=0, tiled=True),
        lax.all_gather(k_weight, "shard", axis=0, tiled=True),
        lax.all_gather(v_weight, "shard", axis=0, tiled=True),
        lax.all_gather(o_weight, "shard", axis=1, tiled=True),
        lax.all_gather(norm2_gain, "shard", axis=0, tiled=True),
        lax.all_gather(gate_weight, "shard", axis=0, tiled=True),
        lax.all_gather(up_weight, "shard", axis=0, tiled=True),
        lax.all_gather(down_weight, "shard", axis=0, tiled=True),
    )
    gain_one, w_query, key_matrix, value_matrix, w_out, gain_two, w_gate, w_up, w_down = params
    gain_one_f = gain_one.astype(jnp.float32)
    gain_two_f = gain_two.astype(jnp.float32)
    cotangent = out_grad[0]
    grad_hidden = back(cotangent, w_down)
    grad_gate = (grad_hidden * upward * sigma * (1.0 + gate * (1.0 - sigma))).astype(jnp.bfloat16)
    grad_upward = (grad_hidden * silu_gate).astype(jnp.bfloat16)
    grad_in_two = back(grad_gate, w_gate) + back(grad_upward, w_up)
    grad_gain_two = jnp.sum(grad_in_two * normed_two, axis=0)
    grad_norm_two = grad_in_two * gain_two_f
    grad_x_one = cotangent.astype(jnp.float32) + inv_two * (
        grad_norm_two - normed_two * jnp.mean(grad_norm_two * normed_two, axis=-1, keepdims=True)
    )
    grad_x_one_b = grad_x_one.astype(jnp.bfloat16)
    attention_gradient = back(grad_x_one_b, w_out).astype(jnp.bfloat16)
    attention_head_gradient = jnp.transpose(
        attention_gradient.reshape(token_count, KEY_VALUE_HEADS, QUERY_PER_KV, HEAD_SIZE),
        (1, 0, 2, 3),
    )
    attention_heads_bf16 = jnp.transpose(
        attended_rows.reshape(token_count, KEY_VALUE_HEADS, QUERY_PER_KV, HEAD_SIZE), (1, 0, 2, 3)
    )
    q_grad, k_grad, v_grad = lax.map(
        partial(head_backward, query_pos=query_pos, key_pos=key_pos),
        (
            query_head_rows,
            key_head_rows,
            value_head_rows,
            log_total,
            attention_head_gradient,
            attention_heads_bf16,
        ),
    )
    key_grad_all = jnp.transpose(k_grad, (1, 0, 2)).reshape(sequence_length_total, KVD)
    value_grad_all = jnp.transpose(v_grad, (1, 0, 2)).reshape(sequence_length_total, KVD)
    local_key_gradient, value_grad_own = (
        lax.psum_scatter(
            key_grad_all.astype(jnp.bfloat16), "shard", scatter_dimension=0, tiled=True
        ).astype(jnp.float32),
        lax.psum_scatter(
            value_grad_all.astype(jnp.bfloat16), "shard", scatter_dimension=0, tiled=True
        ).astype(jnp.float32),
    )
    query_grad = jnp.transpose(q_grad, (1, 0, 2, 3)).reshape(token_count, HQ, HEAD_SIZE)
    grad_q = (
        inverse_rotary(query_grad, cosine_table, sine_table)
        .reshape(token_count, QD)
        .astype(jnp.bfloat16)
    )
    grad_k = (
        inverse_rotary(
            local_key_gradient.reshape(token_count, KEY_VALUE_HEADS, HEAD_SIZE),
            cosine_table,
            sine_table,
        )
        .reshape(token_count, KVD)
        .astype(jnp.bfloat16)
    )
    grad_v = value_grad_own.astype(jnp.bfloat16)
    grad_in_one = back(grad_q, w_query) + back(grad_k, key_matrix) + back(grad_v, value_matrix)
    grad_gain_one = jnp.sum(grad_in_one * normed_one, axis=0)
    grad_norm_one = grad_in_one * gain_one_f
    grad_input = grad_x_one + inv_one * (
        grad_norm_one - normed_one * jnp.mean(grad_norm_one * normed_one, axis=-1, keepdims=True)
    )
    grad_down = outer(hidden_act, cotangent)
    grad_wgate = outer(input_two, grad_gate)
    grad_wup = outer(input_two, grad_upward)
    grad_wout = outer(attended_rows, grad_x_one_b)
    grad_wquery = outer(first_input, grad_q)
    grad_wkey = outer(first_input, grad_k)
    grad_wvalue = outer(first_input, grad_v)
    owned = (
        lax.psum_scatter(
            grad_gain_one.astype(jnp.bfloat16), "shard", scatter_dimension=0, tiled=True
        ).astype(jnp.float32),
        lax.psum_scatter(
            grad_wquery.astype(jnp.bfloat16), "shard", scatter_dimension=0, tiled=True
        ).astype(jnp.float32),
        lax.psum_scatter(
            grad_wkey.astype(jnp.bfloat16), "shard", scatter_dimension=0, tiled=True
        ).astype(jnp.float32),
        lax.psum_scatter(
            grad_wvalue.astype(jnp.bfloat16), "shard", scatter_dimension=0, tiled=True
        ).astype(jnp.float32),
        lax.psum_scatter(
            grad_wout.astype(jnp.bfloat16), "shard", scatter_dimension=1, tiled=True
        ).astype(jnp.float32),
        lax.psum_scatter(
            grad_gain_two.astype(jnp.bfloat16), "shard", scatter_dimension=0, tiled=True
        ).astype(jnp.float32),
        lax.psum_scatter(
            grad_wgate.astype(jnp.bfloat16), "shard", scatter_dimension=0, tiled=True
        ).astype(jnp.float32),
        lax.psum_scatter(
            grad_wup.astype(jnp.bfloat16), "shard", scatter_dimension=0, tiled=True
        ).astype(jnp.float32),
        lax.psum_scatter(
            grad_down.astype(jnp.bfloat16), "shard", scatter_dimension=0, tiled=True
        ).astype(jnp.float32),
    )
    matrices = (owned[1], owned[2], owned[3], owned[4], owned[6], owned[7], owned[8])
    flat_all = jnp.concatenate([matrix.reshape(-1) for matrix in matrices], axis=0)
    share = lax.psum_scatter(
        flat_all.astype(jnp.bfloat16), "rep", scatter_dimension=0, tiled=True
    ).astype(jnp.float32)
    whole = lax.all_gather(share.astype(jnp.bfloat16), "rep", axis=0, tiled=True).astype(
        share.dtype
    )
    gains_sum = lax.psum((owned[0], owned[5]), "rep")
    pieces_back = []
    offset = 0
    for matrix in matrices:
        length = matrix.size
        pieces_back.append(whole[offset : offset + length].reshape(matrix.shape))
        offset = offset + length
    return (
        output[None],
        grad_input[None],
        gains_sum[0],
        pieces_back[0],
        pieces_back[1],
        pieces_back[2],
        pieces_back[3],
        gains_sum[1],
        pieces_back[4],
        pieces_back[5],
        pieces_back[6],
    )


def solution(mesh):
    placed = (
        P("rep", "shard", None),
        P("rep", "shard", None),
        P("shard"),
        P("shard", None),
        P("shard", None),
        P("shard", None),
        P(None, "shard"),
        P("shard"),
        P("shard", None),
        P("shard", None),
        P("shard", None),
    )
    return jax.shard_map(
        local,
        mesh=mesh,
        in_specs=placed,
        out_specs=(
            P("rep", "shard", None),
            P("rep", "shard", None),
            P("shard"),
            P("shard", None),
            P("shard", None),
            P("shard", None),
            P(None, "shard"),
            P("shard"),
            P("shard", None),
            P("shard", None),
            P("shard", None),
        ),
        check_vma=False,
    )
```

profile of v0, /device:TPU:0, one launch (start us, length us, event | category | flops | bytes accessed | tf_op | source)
XLA Modules:
  0.0 838.1 jit_solution(9748543989205862080)
XLA Ops:
  13.9 8.4 all-reduce.7
  22.5 11.5 %all-gather.1 = bf16[4,240,320]{1,2,0:T(8,128)(2,1)S(1)} all-gather(bf16[1,240,320]{1,2,0:T(8,128)(2,1)S(1)} %bitcast.327), channel_id=1, replica_groups=mesh['rep'=8,'shard'=4] {'shard'}, dimensions={0}, use_global_device_ids=true | all-gather | bytes 768000 | tf_op jit(solution)/shard_map/all_gather | solution.py:113
  35.7 6.3 all_gather.49
  42.0 8.0 all-gather
  51.5 8.6 %all_gather.47 = bf16[512,320]{0,1:T(8,128)(2,1)S(1)} all-gather(bf16[128,320]{0,1:T(8,128)(2,1)S(1)} %convolution_convert_fusion.8), channel_id=1, replica_groups=mesh['rep'=8,'shard'=4] {'shard'}, dimensions={0}, use_global_device_ids=true | all-gather | bytes 409600 | tf_op jit(solution)/shard_map/all_gather | solution.py:149
  63.9 4.3 while.30
  71.3 32.4 %all-gather.13.cloned.1.call-done = bf16[960,2560]{1,0:T(8,128)(2,1)} async-done(((bf16[240,2560]{1,0:T(8,128)(2,1)}), bf16[960,2560]{1,0:T(8,128)(2,1)}) %all-gather.13.cloned.1.call-update) | async-done | bytes 4915216 | tf_op jit(solution)/shard_map/all_gather | solution.py:117
  103.7 4.3 fusion.101
  108.0 35.7 %all-gather.15.cloned.1.call-done = bf16[960,2560]{1,0:T(8,128)(2,1)} async-done(((bf16[240,2560]{1,0:T(8,128)(2,1)}), bf16[960,2560]{1,0:T(8,128)(2,1)}) %all-gather.15.cloned.1.call-update) | async-done | bytes 4915216 | tf_op jit(solution)/shard_map/all_gather | solution.py:118
  143.7 4.3 fusion.102
  148.0 35.6 %all-gather.17.cloned.1.call-done = bf16[2560,960]{0,1:T(8,128)(2,1)} async-done(((bf16[640,960]{0,1:T(8,128)(2,1)}), bf16[2560,960]{0,1:T(8,128)(2,1)}) %all-gather.17.cloned.1.call-update) | async-done | bytes 4915216 | tf_op jit(solution)/shard_map/all_gather | solution.py:119
  183.6 5.3 multiply_convert_fusion
  189.0 4.3 fusion.103
  196.7 26.1 %while.31 = (s32[]{:T(128)}, f32[5,128,3,64]{1,3,2,0:T(8,128)S(1)}, bf16[5,512,64]{1,2,0:T(8,128)(2,1)}, bf16[5,512,64]{1,2,0:T(8,128)(2,1)}, bf16[5,512,64]{1,2...) while((s32[]{:T(128)}, f32[5,128,3,64]{1,3,2,0:T(8,128)S(1)}, ...), condition=%wide.region_9.10_spmd.clone.clone, body=%wide.region_7.9_spmd.clone.sunk.clone | while | flops 127762176 | bytes 4536441 | solution.py:211
  226.9 18.9 %reduce-scatter.28.cloned.1.call-done = bf16[128,320]{1,0:T(8,128)(2,1)} async-done(((bf16[512,320]{1,0:T(8,128)(2,1)}), bf16[128,320]{1,0:T(8,128)(2,1)}) %reduce-scatter.28.cloned.1.call-update) | async-done | bytes 81936
  248.6 21.1 %reduce-scatter.30.cloned.1.call-done = bf16[128,320]{1,0:T(8,128)(2,1)} async-done(((bf16[512,320]{1,0:T(8,128)(2,1)}), bf16[128,320]{1,0:T(8,128)(2,1)}) %reduce-scatter.30.cloned.1.call-update) | async-done | bytes 81936
  278.8 4.8 convolution_convert_fusion.2
  284.7 3.6 convolution_convert_fusion.1
  289.5 3.6 convolution_convert_fusion
  293.2 7.9 copy.68
  302.3 19.6 %reduce-scatter.34.cloned.1.call-done = bf16[240,320]{1,0:T(8,128)(2,1)} async-done(((bf16[960,320]{1,0:T(8,128)(2,1)}), bf16[240,320]{1,0:T(8,128)(2,1)}) %reduce-scatter.34.cloned.1.call-update) | async-done | bytes 153616 | tf_op jit(solution)/shard_map/reduce_scatter | solution.py:271
  323.1 32.2 %reduce-scatter.22.cloned.1.call-done = bf16[240,960]{1,0:T(8,128)(2,1)} async-done(((bf16[960,960]{1,0:T(8,128)(2,1)}), bf16[240,960]{1,0:T(8,128)(2,1)}) %reduce-scatter.22.cloned.1.call-update) | async-done | bytes 460816 | tf_op jit(solution)/shard_map/reduce_scatter | solution.py:265
  357.7 31.1 %reduce-scatter.36.cloned.1.call-done = bf16[240,960]{1,0:T(8,128)(2,1)} async-done(((bf16[960,960]{1,0:T(8,128)(2,1)}), bf16[240,960]{1,0:T(8,128)(2,1)}) %reduce-scatter.36.cloned.1.call-update) | async-done | bytes 460816
  393.3 47.2 %reduce-scatter.24.cloned.1.call-done = bf16[240,2560]{1,0:T(8,128)(2,1)} async-done(((bf16[960,2560]{1,0:T(8,128)(2,1)}), bf16[240,2560]{1,0:T(8,128)(2,1)}) %reduce-scatter.24.cloned.1.call-update) | async-done | bytes 1228816 | tf_op jit(solution)/shard_map/reduce_scatter | solution.py:280
  444.5 47.8 %reduce-scatter.26.cloned.1.call-done = bf16[240,2560]{1,0:T(8,128)(2,1)} async-done(((bf16[960,2560]{1,0:T(8,128)(2,1)}), bf16[240,2560]{1,0:T(8,128)(2,1)}) %reduce-scatter.26.cloned.1.call-update) | async-done | bytes 1228816 | tf_op jit(solution)/shard_map/reduce_scatter | solution.py:283
  496.3 49.8 %reduce-scatter.38.cloned.1.call-done = bf16[640,960]{1,0:T(8,128)(2,1)} async-done(((bf16[2560,960]{1,0:T(8,128)(2,1)}), bf16[640,960]{1,0:T(8,128)(2,1)}) %reduce-scatter.38.cloned.1.call-update) | async-done | bytes 1228816 | tf_op jit(solution)/shard_map/reduce_scatter | solution.py:286
  552.1 173.2 %all-reduce.10.cloned.1.call-done = bf16[2457600]{0:T(1024)(128)(2,1)} async-done(((bf16[2457600]{0:T(1024)(128)(2,1)}), bf16[2457600]{0:T(1024)(128)(2,1)}) %all-reduce.10.cloned.1.call-update) | async-done | bytes 4915216
  728.0 4.7 fusion.61
  735.1 6.7 all-reduce.6
  741.9 21.1 %all-reduce.5 = (f32[240]{0:T(256)}, f32[240]{0:T(256)}) all-reduce(f32[240]{0:T(256)S(1)} %get-tuple-element.264, f32[240]{0:T(256)S(1)} %get-tuple-element.263), channel_id=1, replica_groups=mesh['rep'=8,'shard'=4] {'rep'}, use_global_device_ids=true, to_apply=%region_15.16 | all-reduce | flops 480 | bytes 3840 | tf_op jit(solution)/shard_map/psum | solution.py:298
  764.0 45.1 %all-gather.19.cloned.1.call-done = bf16[2457600]{0:T(1024)(128)(2,1)} async-done(((bf16[307200]{0:T(1024)(128)(2,1)}), bf16[2457600]{0:T(1024)(128)(2,1)}) %all-gather.19.cloned.1.call-update) | async-done | bytes 4915216 | tf_op jit(solution)/shard_map/all_gather | solution.py:295
  809.1 5.2 fusion.97
  (279 shorter events, 112.6 us)
Async XLA Ops:
  7.2 53.0 %all-gather.9.cloned.1.call-start = ((), (), s32[]{:S(2)}) async-start(), calls=%async_computation.9 | async-start | bytes 2457600 | tf_op jit(solution)/shard_map/all_gather | solution.py:112
  7.9 60.3 %all-gather.11.cloned.1.call-start = ((), (), s32[]{:S(2)}) async-start(), calls=%async_computation.10 | async-start | bytes 2457600 | tf_op jit(solution)/shard_map/all_gather | solution.py:115
  10.0 12.3 %copy-start = (bf16[1,128,960]{1,2,0:T(8,128)(2,1)S(1)}, bf16[1,128,960]{1,2,0:T(8,128)(2,1)}, u32[]{:S(2)}) copy-start(bf16[1,128,960]{1,2,0:T(8,128)(2,1)} %param.15) | copy-start | bytes 737284
  10.0 12.5 %copy-start.26 = (bf16[240,320]{0,1:T(8,128)(2,1)S(1)}, bf16[240,320]{0,1:T(8,128)(2,1)}, u32[]{:S(2)}) copy-start(bf16[240,320]{0,1:T(8,128)(2,1)} %param.19) | copy-start | bytes 460804
  10.0 93.7 %all-gather.13.cloned.1.call-start = ((), (), s32[]{:S(2)}) async-start(), calls=%async_computation.11 | async-start | bytes 6144000 | tf_op jit(solution)/shard_map/all_gather | solution.py:117
  10.8 132.9 %all-gather.15.cloned.1.call-start = ((), (), s32[]{:S(2)}) async-start(), calls=%async_computation.12 | async-start | bytes 6144000 | tf_op jit(solution)/shard_map/all_gather | solution.py:118
  11.3 172.3 %all-gather.17.cloned.1.call-start = ((), (), s32[]{:S(2)}) async-start(), calls=%async_computation.13 | async-start | bytes 6144000 | tf_op jit(solution)/shard_map/all_gather | solution.py:119
  11.9 233.9 %reduce-scatter.28.cloned.1.call-start = ((), (), s32[]{:S(2)}) async-start(), calls=%async_computation.18 | async-start | bytes 491520
  22.3 40.7 %copy-start.23 = (f32[960]{0:T(1024)}, f32[960]{0:T(1024)S(1)}, u32[]{:S(2)}) copy-start(f32[960]{0:T(1024)S(1)} %convert_element_type.193) | copy-start | bytes 11524
  22.5 40.6 %copy-start.28 = (f32[128]{0:T(128)}, f32[128]{0:T(128)S(1)}, u32[]{:S(2)}) copy-start(f32[128]{0:T(128)S(1)} %add_rsqrt_fusion.1) | copy-start | bytes 1540
  34.0 8.0 copy-start.27
  35.1 15.9 %copy-start.5 = (bf16[960,320]{0,1:T(8,128)(2,1)}, bf16[960,320]{0,1:T(8,128)(2,1)S(1)}, u32[]{:S(2)}) copy-start(bf16[960,320]{0,1:T(8,128)(2,1)S(1)} %reshape.438) | copy-start | bytes 1843204
  51.0 9.1 %copy-start.12 = (bf16[960,320]{0,1:T(8,128)(2,1)}, bf16[960,320]{0,1:T(8,128)(2,1)S(1)}, u32[]{:S(2)}) copy-start(bf16[960,320]{0,1:T(8,128)(2,1)S(1)} %reshape.436) | copy-start | bytes 1843204
  68.2 39.8 %copy-start.19 = (bf16[5,512,64]{1,2,0:T(8,128)(2,1)}, bf16[5,512,64]{1,2,0:T(8,128)(2,1)S(1)}, u32[]{:S(2)}) copy-start(bf16[5,512,64]{1,2,0:T(8,128)(2,1)S(1)} %get-tuple-element.523) | copy-start | bytes 983044
  108.0 75.6 %copy-start.16 = (bf16[1,128,960]{1,2,0:T(8,128)(2,1)S(1)}, bf16[1,128,960]{1,2,0:T(8,128)(2,1)}, u32[]{:S(2)}) copy-start(bf16[1,128,960]{1,2,0:T(8,128)(2,1)} %param.16) | copy-start | bytes 737284
  189.0 4.4 copy-start.1
  222.9 25.7 %copy-start.7 = (bf16[5,128,3,64]{1,3,2,0:T(8,128)(2,1)}, bf16[5,128,3,64]{1,3,2,0:T(8,128)(2,1)S(1)}, u32[]{:S(2)}) copy-start(bf16[5,128,3,64]{1,3,2,0:T(8,128)(2,1)S(1)} %get-tuple-element.509) | copy-start | bytes 737284
  222.9 24.0 %copy-start.24 = (f32[960]{0:T(1024)S(1)}, f32[960]{0:T(1024)}, u32[]{:S(2)}) copy-start(f32[960]{0:T(1024)} %copy-done.23) | copy-start | bytes 11524
  222.9 24.0 %copy-start.29 = (f32[128]{0:T(128)S(1)}, f32[128]{0:T(128)}, u32[]{:S(2)}) copy-start(f32[128]{0:T(128)} %copy-done.28) | copy-start | bytes 1540
  224.9 44.8 %reduce-scatter.30.cloned.1.call-start = ((), (), s32[]{:S(2)}) async-start(), calls=%async_computation.19 | async-start | bytes 491520
  226.9 74.3 %reduce-scatter.32.cloned.1.call-start = ((), (), s32[]{:S(2)}) async-start(), calls=%async_computation.20 | async-start | bytes 921600 | tf_op jit(solution)/shard_map/reduce_scatter | solution.py:268
  248.6 73.3 %reduce-scatter.34.cloned.1.call-start = ((), (), s32[]{:S(2)}) async-start(), calls=%async_computation.21 | async-start | bytes 921600 | tf_op jit(solution)/shard_map/reduce_scatter | solution.py:271
  272.3 83.0 %reduce-scatter.22.cloned.1.call-start = ((), (), s32[]{:S(2)}) async-start(), calls=%async_computation.14 | async-start | bytes 2457600 | tf_op jit(solution)/shard_map/reduce_scatter | solution.py:265
  274.5 114.3 %reduce-scatter.36.cloned.1.call-start = ((), (), s32[]{:S(2)}) async-start(), calls=%async_computation.22 | async-start | bytes 2457600
  278.8 161.7 %reduce-scatter.24.cloned.1.call-start = ((), (), s32[]{:S(2)}) async-start(), calls=%async_computation.15 | async-start | bytes 6144000 | tf_op jit(solution)/shard_map/reduce_scatter | solution.py:280
  283.7 208.7 %reduce-scatter.26.cloned.1.call-start = ((), (), s32[]{:S(2)}) async-start(), calls=%async_computation.16 | async-start | bytes 6144000 | tf_op jit(solution)/shard_map/reduce_scatter | solution.py:283
  288.4 257.7 %reduce-scatter.38.cloned.1.call-start = ((), (), s32[]{:S(2)}) async-start(), calls=%async_computation.23 | async-start | bytes 6553600 | tf_op jit(solution)/shard_map/reduce_scatter | solution.py:286
  301.0 424.2 %all-reduce.10.cloned.1.call-start = ((), (), s32[]{:S(2)}) async-start(), calls=%async_computation.24 | async-start | bytes 9830400
  550.3 258.8 %all-gather.19.cloned.1.call-start = ((), (), s32[]{:S(2)}) async-start(), calls=%async_computation.17 | async-start | bytes 5529600 | tf_op jit(solution)/shard_map/all_gather | solution.py:295
  727.9 4.8 copy-start.6
  727.9 5.2 copy-start.13
  727.9 5.2 copy-start.22
  (20 other events, 42.5 us)
Sparse Core Ops, SparseCore 0:
  9.5 28.1 all-gather.8
  39.8 23.5 all-gather.10
  65.0 38.6 all-gather.12
  105.1 38.5 all-gather.14
  145.1 38.4 all-gather.16
  225.0 20.7 reduce-scatter.27
  248.9 20.7 reduce-scatter.29
  272.8 22.9 reduce-scatter.31
  298.9 22.9 reduce-scatter.33
  324.9 30.3 reduce-scatter.21
  358.4 30.3 reduce-scatter.35
  391.3 49.2 reduce-scatter.23
  443.1 49.2 reduce-scatter.25
  494.7 51.3 reduce-scatter.37
  550.4 174.8 all-reduce.9
  727.9 81.1 all-gather.18
where the time goes:
time: 840 us; the launch traced here: 838 us
  waiting for transfers between devices  592 us (70%)
  matrix products  77.6 us (9%)
  local copies, waits for them, and re-layouts  75.7 us (9%)
  blocking collectives  70.6 us (8%)
  between operations  16.6 us (2%)
    unnamed x20, waiting for transfers between devices  247 us
    reduce_scatter x1, waiting for transfers between devices, local(): lax.psum_scatter(grad_down.astype(jnp.bfloat16), 'shard', scatter_dimensi...  49.8 us
    reduce_scatter x1, waiting for transfers between devices, local(): lax.psum_scatter(grad_wup.astype(jnp.bfloat16), 'shard', scatter_dimensio...  47.8 us
    reduce_scatter x1, waiting for transfers between devices, local(): lax.psum_scatter(grad_wgate.astype(jnp.bfloat16), 'shard', scatter_dimens...  47.2 us
    all_gather x1, waiting for transfers between devices, local(): lax.all_gather(share.astype(jnp.bfloat16), 'rep', axis=0, tiled=True)  45.1 us
    unnamed x99, local copies, waits for them, and re-layouts  38.3 us
    all_gather x1, waiting for transfers between devices, local(): lax.all_gather(up_weight, 'shard', axis=0, tiled=True)  35.7 us
    all_gather x1, waiting for transfers between devices, local(): lax.all_gather(down_weight, 'shard', axis=0, tiled=True)  35.6 us
  transfers between devices with their start and end apart: 16, of which 13 were waited for; matrix products, arithmetic and copies ran while one was open for 10% of the time, Pallas kernels for 0%

commit v1 on v0

--- a/solution.py
+++ b/solution.py
@@ -14,6 +14,22 @@
 SCALE = 0.125
 NEGATIVE = -1e30
 THETA = 10000.0
+
+
+def gather_around(x, axis, dim):
+    ways, here, step = (lax.axis_size(axis), lax.axis_index(axis), x.shape[dim])
+    shape = [n * ways if d == dim else n for d, n in enumerate(x.shape)]
+    full = lax.dynamic_update_slice_in_dim(jnp.zeros(shape, x.dtype), x, here * step, axis=dim)
+    going_up = going_down = x
+    for far in range(1, ways // 2 + 1):
+        going_up = lax.ppermute(going_up, axis, [(d, (d + 1) % ways) for d in range(ways)])
+        full = lax.dynamic_update_slice_in_dim(full, going_up, (here - far) % ways * step, axis=dim)
+        if 2 * far < ways:
+            going_down = lax.ppermute(going_down, axis, [(d, (d - 1) % ways) for d in range(ways)])
+            full = lax.dynamic_update_slice_in_dim(
+                full, going_down, (here + far) % ways * step, axis=dim
+            )
+    return full
 
 
 def rms_inverse(rows):
@@ -292,9 +308,7 @@
     share = lax.psum_scatter(
         flat_all.astype(jnp.bfloat16), "rep", scatter_dimension=0, tiled=True
     ).astype(jnp.float32)
-    whole = lax.all_gather(share.astype(jnp.bfloat16), "rep", axis=0, tiled=True).astype(
-        share.dtype
-    )
+    whole = gather_around(share.astype(jnp.bfloat16), "rep", 0).astype(share.dtype)
     gains_sum = lax.psum((owned[0], owned[5]), "rep")
     pieces_back = []
     offset = 0

time: 840 us -> 975 us (1.16); the launches traced: 838 us -> 961 us
  local copies, waits for them, and re-layouts: 75.7 us -> 156 us
  waiting for transfers between devices: 592 us -> 609 us
  starting transfers between devices: 1.13 us -> 17.8 us
    dynamic_update_slice x0 -> x8, local copies, waits for them, and re-layouts: none -> 74.6 us  [the longest x4 41.4 us: gather_around(): lax.dynamic_update_slice_in_dim(full, going_up, (here - far) % ways * ste...]
    ppermute x0 -> x7, waiting for transfers between devices: none -> 63 us  [the longest x4 63 us: gather_around(): lax.ppermute(going_up, axis, [(d, (d + 1) % ways) for d in range(ways)])]
    all_gather x1 -> x0, waiting for transfers between devices: 45.1 us -> none  [local(): lax.all_gather(share.astype(jnp.bfloat16), 'rep', axis=0, tiled=True)]
    ppermute x0 -> x7, starting transfers between devices: none -> 17 us  [the longest x4 9.12 us: gather_around(): lax.ppermute(going_up, axis, [(d, (d + 1) % ways) for d in range(ways)])]
    unnamed x99 -> x100, local copies, waits for them, and re-layouts: 38.3 us -> 33.3 us
    unnamed x20 -> x19, waiting for transfers between devices: 247 us -> 248 us
  transfers between devices with their start and end apart: 16 -> 22, of which waited for: 13 -> 15; matrix products, arithmetic and copies ran while one was open for 10% -> 16% of each run, Pallas kernels for 0% -> 0%
where the time goes in v1:
time: 975 us; the launch traced here: 961 us
  waiting for transfers between devices  609 us (62%)
  local copies, waits for them, and re-layouts  156 us (16%)
  matrix products  85.5 us (9%)
  blocking collectives  69 us (7%)
  starting transfers between devices  17.8 us (2%)
  between operations  16.9 us (2%)
    unnamed x19, waiting for transfers between devices  248 us
    ppermute x4, waiting for transfers between devices, gather_around(): lax.ppermute(going_up, axis, [(d, (d + 1) % ways) for d in range(ways)])  63 us
    reduce_scatter x1, waiting for transfers between devices, local(): lax.psum_scatter(grad_down.astype(jnp.bfloat16), 'shard', scatter_dimensi...  49.8 us
    reduce_scatter x1, waiting for transfers between devices, local(): lax.psum_scatter(grad_wup.astype(jnp.bfloat16), 'shard', scatter_dimensio...  47.8 us
    reduce_scatter x1, waiting for transfers between devices, local(): lax.psum_scatter(grad_wgate.astype(jnp.bfloat16), 'shard', scatter_dimens...  47.2 us
    dynamic_update_slice x4, local copies, waits for them, and re-layouts, gather_around(): lax.dynamic_update_slice_in_dim(full, going_up, (here - far) % ways * ste...  41.4 us
    all_gather x1, waiting for transfers between devices, local(): lax.all_gather(up_weight, 'shard', axis=0, tiled=True)  35.7 us
    all_gather x1, waiting for transfers between devices, local(): lax.all_gather(down_weight, 'shard', axis=0, tiled=True)  35.6 us
  transfers between devices with their start and end apart: 22, of which 15 were waited for; matrix products, arithmetic and copies ran while one was open for 16% of the time, Pallas kernels for 0%

profile of v1, /device:TPU:0, one launch (start us, length us, event | category | flops | bytes accessed | tf_op | source)
XLA Modules:
  0.0 961.2 jit_solution(4228612902017331762)
XLA Ops:
  13.9 8.4 all-reduce.7
  22.5 11.5 %all-gather.1 = bf16[4,240,320]{1,2,0:T(8,128)(2,1)S(1)} all-gather(bf16[1,240,320]{1,2,0:T(8,128)(2,1)S(1)} %bitcast.327), channel_id=1, replica_groups=mesh['rep'=8,'shard'=4] {'shard'}, dimensions={0}, use_global_device_ids=true | all-gather | bytes 768000 | tf_op jit(solution)/shard_map/all_gather | solution.py:129
  35.7 6.3 all_gather.46
  42.0 8.0 all-gather
  51.5 8.9 all_gather.44
  64.2 7.1 while.30
  74.7 29.0 %all-gather.12.cloned.1.call-done = bf16[960,2560]{1,0:T(8,128)(2,1)} async-done(((bf16[240,2560]{1,0:T(8,128)(2,1)}), bf16[960,2560]{1,0:T(8,128)(2,1)}) %all-gather.12.cloned.1.call-update) | async-done | bytes 4915216 | tf_op jit(solution)/shard_map/all_gather | solution.py:133
  108.0 35.7 %all-gather.14.cloned.1.call-done = bf16[960,2560]{1,0:T(8,128)(2,1)} async-done(((bf16[240,2560]{1,0:T(8,128)(2,1)}), bf16[960,2560]{1,0:T(8,128)(2,1)}) %all-gather.14.cloned.1.call-update) | async-done | bytes 4915216 | tf_op jit(solution)/shard_map/all_gather | solution.py:134
  148.1 35.6 %all-gather.16.cloned.1.call-done = bf16[2560,960]{0,1:T(8,128)(2,1)} async-done(((bf16[640,960]{0,1:T(8,128)(2,1)}), bf16[2560,960]{0,1:T(8,128)(2,1)}) %all-gather.16.cloned.1.call-update) | async-done | bytes 4915216 | tf_op jit(solution)/shard_map/all_gather | solution.py:135
  196.8 36.9 %while.31 = (s32[]{:T(128)}, f32[5,128,3,64]{1,3,2,0:T(8,128)}, bf16[5,512,64]{1,2,0:T(8,128)(2,1)}, bf16[5,512,64]{1,2,0:T(8,128)(2,1)}, bf16[5,512,64]{1,2,0:T...) while((s32[]{:T(128)}, f32[5,128,3,64]{1,3,2,0:T(8,128)}, ...), condition=%wide.region_9.10_spmd.clone.clone, body=%wide.region_7.9_spmd.clone.sunk.clone | while | flops 127762176 | bytes 4536441 | solution.py:227
  237.7 19.0 %reduce-scatter.28.cloned.1.call-done = bf16[128,320]{1,0:T(8,128)(2,1)} async-done(((bf16[512,320]{1,0:T(8,128)(2,1)}), bf16[128,320]{1,0:T(8,128)(2,1)}) %reduce-scatter.28.cloned.1.call-update) | async-done | bytes 81936
  259.4 21.1 %reduce-scatter.30.cloned.1.call-done = bf16[128,320]{1,0:T(8,128)(2,1)} async-done(((bf16[512,320]{1,0:T(8,128)(2,1)}), bf16[128,320]{1,0:T(8,128)(2,1)}) %reduce-scatter.30.cloned.1.call-update) | async-done | bytes 81936
  302.0 7.9 copy.68
  311.2 21.5 %reduce-scatter.34.cloned.1.call-done = bf16[240,320]{1,0:T(8,128)(2,1)} async-done(((bf16[960,320]{1,0:T(8,128)(2,1)}), bf16[240,320]{1,0:T(8,128)(2,1)}) %reduce-scatter.34.cloned.1.call-update) | async-done | bytes 153616 | tf_op jit(solution)/shard_map/reduce_scatter | solution.py:287
  333.9 32.2 %reduce-scatter.22.cloned.1.call-done = bf16[240,960]{1,0:T(8,128)(2,1)} async-done(((bf16[960,960]{1,0:T(8,128)(2,1)}), bf16[240,960]{1,0:T(8,128)(2,1)}) %reduce-scatter.22.cloned.1.call-update) | async-done | bytes 460816 | tf_op jit(solution)/shard_map/reduce_scatter | solution.py:281
  368.5 31.1 %reduce-scatter.36.cloned.1.call-done = bf16[240,960]{1,0:T(8,128)(2,1)} async-done(((bf16[960,960]{1,0:T(8,128)(2,1)}), bf16[240,960]{1,0:T(8,128)(2,1)}) %reduce-scatter.36.cloned.1.call-update) | async-done | bytes 460816
  404.1 47.2 %reduce-scatter.24.cloned.1.call-done = bf16[240,2560]{1,0:T(8,128)(2,1)} async-done(((bf16[960,2560]{1,0:T(8,128)(2,1)}), bf16[240,2560]{1,0:T(8,128)(2,1)}) %reduce-scatter.24.cloned.1.call-update) | async-done | bytes 1228816 | tf_op jit(solution)/shard_map/reduce_scatter | solution.py:296
  455.3 47.8 %reduce-scatter.26.cloned.1.call-done = bf16[240,2560]{1,0:T(8,128)(2,1)} async-done(((bf16[960,2560]{1,0:T(8,128)(2,1)}), bf16[240,2560]{1,0:T(8,128)(2,1)}) %reduce-scatter.26.cloned.1.call-update) | async-done | bytes 1228816 | tf_op jit(solution)/shard_map/reduce_scatter | solution.py:299
  507.1 49.8 %reduce-scatter.38.cloned.1.call-done = bf16[640,960]{1,0:T(8,128)(2,1)} async-done(((bf16[2560,960]{1,0:T(8,128)(2,1)}), bf16[640,960]{1,0:T(8,128)(2,1)}) %reduce-scatter.38.cloned.1.call-update) | async-done | bytes 1228816 | tf_op jit(solution)/shard_map/reduce_scatter | solution.py:302
  562.3 173.7 %all-reduce.10.cloned.1.call-done = bf16[2457600]{0:T(1024)(128)(2,1)} async-done(((bf16[2457600]{0:T(1024)(128)(2,1)}), bf16[2457600]{0:T(1024)(128)(2,1)}) %all-reduce.10.cloned.1.call-update) | async-done | bytes 4915216
  745.6 23.1 %collective-permute-done = bf16[307200]{0:T(1024)(128)(2,1)} collective-permute-done((bf16[307200]{0:T(1024)(128)(2,1)}, bf16[307200]{0:T(1024)(128)(2,1)}, u32[]{:S(2)}, u32[]{:S(2)}) %collective-permute-start) | collective-permute-done | bytes 614432 | tf_op jit(solution)/shard_map/ppermute | solution.py:25
  774.2 22.8 %collective-permute-done.2 = bf16[307200]{0:T(1024)(128)(2,1)} collective-permute-done((bf16[307200]{0:T(1024)(128)(2,1)}, bf16[307200]{0:T(1024)(128)(2,1)}, u32[]{:S(2)}, u32[]{:S(2)}) %collective-permute-start.2) | collective-permute-done | bytes 614432 | tf_op jit(solution)/shard_map/ppermute | solution.py:25
  807.7 17.1 %collective-permute-done.4 = bf16[307200]{0:T(1024)(128)(2,1)} collective-permute-done((bf16[307200]{0:T(1024)(128)(2,1)}, bf16[307200]{0:T(1024)(128)(2,1)}, u32[]{:S(2)}, u32[]{:S(2)}) %collective-permute-start.4) | collective-permute-done | bytes 614432 | tf_op jit(solution)/shard_map/ppermute | solution.py:25
  828.1 6.1 all-reduce.6
  834.2 19.9 %all-reduce.5 = (f32[240]{0:T(256)}, f32[240]{0:T(256)}) all-reduce(f32[240]{0:T(256)S(1)} %get-tuple-element.266, f32[240]{0:T(256)S(1)} %get-tuple-element.265), channel_id=1, replica_groups=mesh['rep'=8,'shard'=4] {'rep'}, use_global_device_ids=true, to_apply=%region_15.16 | all-reduce | flops 480 | bytes 3840 | tf_op jit(solution)/shard_map/psum | solution.py:312
  855.1 10.4 %dynamic_update_slice.43 = bf16[2457600]{0:T(1024)(128)(2,1)} dynamic-update-slice(bf16[2457600]{0:T(1024)(128)(2,1)} %get-tuple-element.235, bf16[307200]{0:T(1024)(128)(2,1)} %collective-permute-done, s32[]{:T(128)S(6)} %select_n.89) | dynamic-update-slice | bytes 1228804 | tf_op jit(solution)/shard_map/dynamic_update_slice | solution.py:26
  865.5 10.4 %dynamic_update_slice.44 = bf16[2457600]{0:T(1024)(128)(2,1)} dynamic-update-slice(bf16[2457600]{0:T(1024)(128)(2,1)} %dynamic_update_slice.43, bf16[307200]{0:T(1024)(128)(2,1)} %collective-permute-done.1, s32[]{:T(128)S(6)} %select_n.91) | dynamic-update-slice | bytes 1228804 | tf_op jit(solution)/shard_map/dynamic_update_slice | solution.py:29
  875.8 10.3 %dynamic_update_slice.45 = bf16[2457600]{0:T(1024)(128)(2,1)} dynamic-update-slice(bf16[2457600]{0:T(1024)(128)(2,1)} %dynamic_update_slice.44, bf16[307200]{0:T(1024)(128)(2,1)} %collective-permute-done.2, s32[]{:T(128)S(6)} %select_n.93) | dynamic-update-slice | bytes 1228804 | tf_op jit(solution)/shard_map/dynamic_update_slice | solution.py:26
  886.2 10.3 %dynamic_update_slice.46 = bf16[2457600]{0:T(1024)(128)(2,1)} dynamic-update-slice(bf16[2457600]{0:T(1024)(128)(2,1)} %dynamic_update_slice.45, bf16[307200]{0:T(1024)(128)(2,1)} %collective-permute-done.3, s32[]{:T(128)S(6)} %select_n.95) | dynamic-update-slice | bytes 1228804 | tf_op jit(solution)/shard_map/dynamic_update_slice | solution.py:29
  896.5 10.4 %dynamic_update_slice.47 = bf16[2457600]{0:T(1024)(128)(2,1)} dynamic-update-slice(bf16[2457600]{0:T(1024)(128)(2,1)} %dynamic_update_slice.46, bf16[307200]{0:T(1024)(128)(2,1)} %collective-permute-done.4, s32[]{:T(128)S(6)} %select_n.97) | dynamic-update-slice | bytes 1228804 | tf_op jit(solution)/shard_map/dynamic_update_slice | solution.py:26
  906.9 10.3 %dynamic_update_slice.48 = bf16[2457600]{0:T(1024)(128)(2,1)} dynamic-update-slice(bf16[2457600]{0:T(1024)(128)(2,1)} %dynamic_update_slice.47, bf16[307200]{0:T(1024)(128)(2,1)} %collective-permute-done.5, s32[]{:T(128)S(6)} %select_n.99) | dynamic-update-slice | bytes 1228804 | tf_op jit(solution)/shard_map/dynamic_update_slice | solution.py:29
  917.2 10.4 %dynamic_update_slice.49 = bf16[2457600]{0:T(1024)(128)(2,1)} dynamic-update-slice(bf16[2457600]{0:T(1024)(128)(2,1)} %dynamic_update_slice.48, bf16[307200]{0:T(1024)(128)(2,1)} %collective-permute-done.6, s32[]{:T(128)S(6)} %select_n.101) | dynamic-update-slice | bytes 1228804 | tf_op jit(solution)/shard_map/dynamic_update_slice | solution.py:26
  (300 shorter events, 187.8 us)
Async XLA Ops:
  7.2 53.2 %all-gather.8.cloned.1.call-start = ((), (), s32[]{:S(2)}) async-start(), calls=%async_computation.9 | async-start | bytes 2457600 | tf_op jit(solution)/shard_map/all_gather | solution.py:128
  8.0 63.4 %all-gather.10.cloned.1.call-start = ((), (), s32[]{:S(2)}) async-start(), calls=%async_computation.10 | async-start | bytes 2457600 | tf_op jit(solution)/shard_map/all_gather | solution.py:131
  10.1 93.6 %all-gather.12.cloned.1.call-start = ((), (), s32[]{:S(2)}) async-start(), calls=%async_computation.11 | async-start | bytes 6144000 | tf_op jit(solution)/shard_map/all_gather | solution.py:133
  10.8 132.9 %all-gather.14.cloned.1.call-start = ((), (), s32[]{:S(2)}) async-start(), calls=%async_computation.12 | async-start | bytes 6144000 | tf_op jit(solution)/shard_map/all_gather | solution.py:134
  11.4 172.3 %all-gather.16.cloned.1.call-start = ((), (), s32[]{:S(2)}) async-start(), calls=%async_computation.13 | async-start | bytes 6144000 | tf_op jit(solution)/shard_map/all_gather | solution.py:135
  12.0 244.7 %reduce-scatter.28.cloned.1.call-start = ((), (), s32[]{:S(2)}) async-start(), calls=%async_computation.17 | async-start | bytes 491520
  74.7 109.0 %copy-start.17 = (bf16[1,128,960]{1,2,0:T(8,128)(2,1)S(1)}, bf16[1,128,960]{1,2,0:T(8,128)(2,1)}, u32[]{:S(2)}) copy-start(bf16[1,128,960]{1,2,0:T(8,128)(2,1)} %param.16) | copy-start | bytes 737284
  196.7 61.0 %copy-start.25 = (f32[960]{0:T(1024)S(1)}, f32[960]{0:T(1024)}, u32[]{:S(2)}) copy-start(f32[960]{0:T(1024)} %copy-done.24) | copy-start | bytes 11524
  196.8 61.0 %copy-start.30 = (f32[128]{0:T(128)S(1)}, f32[128]{0:T(128)}, u32[]{:S(2)}) copy-start(f32[128]{0:T(128)} %copy-done.29) | copy-start | bytes 1540
  233.6 49.6 %copy-start.7 = (bf16[5,128,3,64]{1,3,2,0:T(8,128)(2,1)}, bf16[5,128,3,64]{1,3,2,0:T(8,128)(2,1)S(1)}, u32[]{:S(2)}) copy-start(bf16[5,128,3,64]{1,3,2,0:T(8,128)(2,1)S(1)} %get-tuple-element.509) | copy-start | bytes 737284
  235.7 44.9 %reduce-scatter.30.cloned.1.call-start = ((), (), s32[]{:S(2)}) async-start(), calls=%async_computation.18 | async-start | bytes 491520
  237.6 72.4 %reduce-scatter.32.cloned.1.call-start = ((), (), s32[]{:S(2)}) async-start(), calls=%async_computation.19 | async-start | bytes 921600 | tf_op jit(solution)/shard_map/reduce_scatter | solution.py:284
  259.4 73.3 %reduce-scatter.34.cloned.1.call-start = ((), (), s32[]{:S(2)}) async-start(), calls=%async_computation.20 | async-start | bytes 921600 | tf_op jit(solution)/shard_map/reduce_scatter | solution.py:287
  283.1 83.0 %reduce-scatter.22.cloned.1.call-start = ((), (), s32[]{:S(2)}) async-start(), calls=%async_computation.14 | async-start | bytes 2457600 | tf_op jit(solution)/shard_map/reduce_scatter | solution.py:281
  285.3 114.3 %reduce-scatter.36.cloned.1.call-start = ((), (), s32[]{:S(2)}) async-start(), calls=%async_computation.21 | async-start | bytes 2457600
  289.6 161.7 %reduce-scatter.24.cloned.1.call-start = ((), (), s32[]{:S(2)}) async-start(), calls=%async_computation.15 | async-start | bytes 6144000 | tf_op jit(solution)/shard_map/reduce_scatter | solution.py:296
  294.6 208.6 %reduce-scatter.26.cloned.1.call-start = ((), (), s32[]{:S(2)}) async-start(), calls=%async_computation.16 | async-start | bytes 6144000 | tf_op jit(solution)/shard_map/reduce_scatter | solution.py:299
  298.2 258.6 %reduce-scatter.38.cloned.1.call-start = ((), (), s32[]{:S(2)}) async-start(), calls=%async_computation.22 | async-start | bytes 6553600 | tf_op jit(solution)/shard_map/reduce_scatter | solution.py:302
  309.9 426.1 %all-reduce.10.cloned.1.call-start = ((), (), s32[]{:S(2)}) async-start(), calls=%async_computation.23 | async-start | bytes 9830400
  507.1 54.0 %copy-start.36 = (u32[32]{0:T(128)S(1)}, u32[32]{0:T(128)}, u32[]{:S(2)}) copy-start(u32[32]{0:T(128)} %constant.158) | copy-start | bytes 388
  740.8 86.5 %copy-start.3 = (bf16[960,960]{1,0:T(8,128)(2,1)S(1)}, bf16[960,960]{1,0:T(8,128)(2,1)}, u32[]{:S(2)}) copy-start(bf16[960,960]{1,0:T(8,128)(2,1)} %all-gather.8.cloned.1.call-done) | copy-start | bytes 5529604
  740.8 86.5 %copy-start.16 = (bf16[128,15,64]{0,2,1:T(8,128)(2,1)S(1)}, bf16[128,15,64]{0,2,1:T(8,128)(2,1)}, u32[]{:S(2)}) copy-start(bf16[128,15,64]{0,2,1:T(8,128)(2,1)} %copy-done.15) | copy-start | bytes 737284
  740.8 86.5 %copy-start.26 = (f32[960]{0:T(1024)S(1)}, f32[960]{0:T(1024)}, u32[]{:S(2)}) copy-start(f32[960]{0:T(1024)} %copy-done.24) | copy-start | bytes 11524
  740.8 86.5 %copy-start.31 = (f32[128]{0:T(128)S(1)}, f32[128]{0:T(128)}, u32[]{:S(2)}) copy-start(f32[128]{0:T(128)} %copy-done.29) | copy-start | bytes 1540
  740.8 27.9 %collective-permute-start = (bf16[307200]{0:T(1024)(128)(2,1)}, bf16[307200]{0:T(1024)(128)(2,1)}, u32[]{:S(2)}, u32[]{:S(2)}) collective-permute-start(bf16[307200]{0:T(1024)(128)(2,1)} %get-tuple-element.236), channel_id=1, source_target_pairs={{0,4},{4,8},{8,12},{12,16},{16,20},{20,24},{24,28},{28,0},{1,5},{5... | collective-permute-start | bytes 1843208 | tf_op jit(solution)/shard_map/ppermute | solution.py:25
  742.3 29.6 %collective-permute-start.1 = (bf16[307200]{0:T(1024)(128)(2,1)}, bf16[307200]{0:T(1024)(128)(2,1)}, u32[]{:S(2)}, u32[]{:S(2)}) collective-permute-start(bf16[307200]{0:T(1024)(128)(2,1)} %get-tuple-element.236), channel_id=1, source_target_pairs={{0,28},{4,0},{8,4},{12,8},{16,12},{20,16},{24,20},{28,24},{1,29},{... | collective-permute-start | bytes 1843208 | tf_op jit(solution)/shard_map/ppermute | solution.py:28
  768.7 28.3 %collective-permute-start.2 = (bf16[307200]{0:T(1024)(128)(2,1)}, bf16[307200]{0:T(1024)(128)(2,1)}, u32[]{:S(2)}, u32[]{:S(2)}) collective-permute-start(bf16[307200]{0:T(1024)(128)(2,1)} %collective-permute-done), channel_id=1, source_target_pairs={{0,4},{4,8},{8,12},{12,16},{16,20},{20,24},{24,28},{28,0},{1,5},{5... | collective-permute-start | bytes 1843208 | tf_op jit(solution)/shard_map/ppermute | solution.py:25
  771.9 56.2 %copy-start.32 = (bf16[960]{0:T(1024)(128)(2,1)S(1)}, bf16[960]{0:T(1024)(128)(2,1)}, u32[]{:S(2)}) copy-start(bf16[960]{0:T(1024)(128)(2,1)} %get-tuple-element.189) | copy-start | bytes 5764
  771.9 33.5 %collective-permute-start.3 = (bf16[307200]{0:T(1024)(128)(2,1)}, bf16[307200]{0:T(1024)(128)(2,1)}, u32[]{:S(2)}, u32[]{:S(2)}) collective-permute-start(bf16[307200]{0:T(1024)(128)(2,1)} %collective-permute-done.1), channel_id=1, source_target_pairs={{0,28},{4,0},{8,4},{12,8},{16,12},{20,16},{24,20},{28,24},{1,29},{... | collective-permute-start | bytes 1843208 | tf_op jit(solution)/shard_map/ppermute | solution.py:28
  797.0 27.8 %collective-permute-start.4 = (bf16[307200]{0:T(1024)(128)(2,1)}, bf16[307200]{0:T(1024)(128)(2,1)}, u32[]{:S(2)}, u32[]{:S(2)}) collective-permute-start(bf16[307200]{0:T(1024)(128)(2,1)} %collective-permute-done.2), channel_id=1, source_target_pairs={{0,4},{4,8},{8,12},{12,16},{16,20},{20,24},{24,28},{28,0},{1,5},{5... | collective-permute-start | bytes 1843208 | tf_op jit(solution)/shard_map/ppermute | solution.py:25
  805.4 101.4 %collective-permute-start.5 = (bf16[307200]{0:T(1024)(128)(2,1)}, bf16[307200]{0:T(1024)(128)(2,1)}, u32[]{:S(2)}, u32[]{:S(2)}) collective-permute-start(bf16[307200]{0:T(1024)(128)(2,1)} %collective-permute-done.3), channel_id=1, source_target_pairs={{0,28},{4,0},{8,4},{12,8},{16,12},{20,16},{24,20},{28,24},{1,29},{... | collective-permute-start | bytes 1843208 | tf_op jit(solution)/shard_map/ppermute | solution.py:28
  824.8 92.4 %collective-permute-start.6 = (bf16[307200]{0:T(1024)(128)(2,1)}, bf16[307200]{0:T(1024)(128)(2,1)}, u32[]{:S(2)}, u32[]{:S(2)}) collective-permute-start(bf16[307200]{0:T(1024)(128)(2,1)} %collective-permute-done.4), channel_id=1, source_target_pairs={{0,4},{4,8},{8,12},{12,16},{16,20},{20,24},{24,28},{28,0},{1,5},{5... | collective-permute-start | bytes 1843208 | tf_op jit(solution)/shard_map/ppermute | solution.py:25
  (27 other events, 430.3 us)
Sparse Core Ops, SparseCore 0:
  9.6 28.1 all-gather.7
  39.9 23.5 all-gather.9
  65.1 38.5 all-gather.11
  105.1 38.5 all-gather.13
  145.1 38.4 all-gather.15
  235.8 20.8 reduce-scatter.27
  259.7 20.8 reduce-scatter.29
  283.7 22.9 reduce-scatter.31
  309.7 22.9 reduce-scatter.33
  335.7 30.3 reduce-scatter.21
  369.2 30.3 reduce-scatter.35
  402.1 49.2 reduce-scatter.23
  453.9 49.1 reduce-scatter.25
  505.5 51.3 reduce-scatter.37
  561.2 174.8 all-reduce.9
